TPU v7x, 32 devices: a whole 2x2x4 slice. The times are simulated.
32 devices in a mesh: cond: 4 (over y, core), seq: 8 (over z, x).
Axes of the slice: x: 2, y: 2, z: 4, core: 2. Of those that a mesh axis runs over, the one named last changes fastest.
Arguments:
- inputs: bfloat16 [4, 4096, 1024], P(None, 'seq', 'cond'), may hold values from -100 to 100
- coarse_ids: int32 [4, 1024], P(None, 'seq'), may hold values from 0 to 2047
- segment_ids: int32 [4, 4096], P(None, 'seq'), may hold values from 0 to 31, never falling along the last dimension, each value on 1 to 256 neighbouring positions
- cotangent: bfloat16 [4, 4096, 1024], P(None, 'seq', 'cond'), may hold values from -6 to 6
- embed_table: bfloat16 [2048, 1024], P('seq', 'cond'), may hold values from -6 to 6
- conv_weight: bfloat16 [3, 1024, 1024], P(None, 'cond', 'seq'), may hold values from -0.109375 to 0.109375
- res_weight: bfloat16 [1024, 1024], P('seq', 'cond'), may hold values from -0.1875 to 0.1875
- up_weight: bfloat16 [1024, 4096], P('cond', 'seq'), may hold values from -0.1875 to 0.1875
- gain_one: bfloat16 [1024], P(('cond', 'seq')), may hold values from 0.5 to 1.5
- shift_one: bfloat16 [1024], P(('cond', 'seq')), may hold values from -2 to 2
- qkv_weight: bfloat16 [1024, 3, 1024], P('seq', None, 'cond'), may hold values from -0.1875 to 0.1875
- out_weight: bfloat16 [1024, 1024], P('cond', 'seq'), may hold values from -0.5 to 0.5
- gain_two: bfloat16 [1024], P(('cond', 'seq')), may hold values from 0.5 to 1.5
- shift_two: bfloat16 [1024], P(('cond', 'seq')), may hold values from -2 to 2
- in_weight: bfloat16 [1024, 4096], P('seq', 'cond'), may hold values from -0.1875 to 0.1875
- down_weight: bfloat16 [4096, 1024], P('cond', 'seq'), may hold values from -0.09375 to 0.09375
Outputs:
- activation: bfloat16 [4, 4096, 1024], P(None, 'seq', 'cond')
- input_grad: bfloat16 [4, 4096, 1024], P(None, 'seq', 'cond')
- grad_table: float32 [2048, 1024], P('seq', 'cond')
- grad_conv: float32 [3, 1024, 1024], P(None, 'cond', 'seq')
- grad_res: float32 [1024, 1024], P('seq', 'cond')
- grad_up: float32 [1024, 4096], P('cond', 'seq')
- grad_gain_one: float32 [1024], P(('cond', 'seq'))
- grad_shift_one: float32 [1024], P(('cond', 'seq'))
- grad_qkv: float32 [1024, 3, 1024], P('seq', None, 'cond')
- grad_out: float32 [1024, 1024], P('cond', 'seq')
- grad_gain_two: float32 [1024], P(('cond', 'seq'))
- grad_shift_two: float32 [1024], P(('cond', 'seq'))
- grad_in: float32 [1024, 4096], P('seq', 'cond')
- grad_down: float32 [4096, 1024], P('cond', 'seq')
All inputs are finite; a program needn't handle non-finite values.
Results may differ from a plain program's by a relative error of at most 0.02.
Values may be sent and summed in bfloat16 or wider, within the bound.
No kernel may reach another device: no remote copies, remote signals or barrier semaphores. Data moves between devices by JAX's collectives and lax.ppermute only.
A program may use at most 112 MiB of HBM per device.

v0:
```python
import math
import jax
import jax.numpy as jnp
from jax import lax
from jax.sharding import PartitionSpec as P

HEAD = 64
ROW = 64
CONV_DILATION = 27
EPSILON = 1e-05
NEG_FILL = -1e30


def extended(cells, sides, width):
    for axis, dim in sides:
        count = lax.axis_size(axis)
        ends = count - 1
        head = lax.slice_in_dim(cells, 0, width, axis=dim)
        tail = lax.slice_in_dim(cells, cells.shape[dim] - width, cells.shape[dim], axis=dim)
        cells = jnp.concatenate(
            [
                lax.ppermute(tail, axis, [(i, (i + 1) % count) for i in range(ends)]),
                cells,
                lax.ppermute(head, axis, [((i + 1) % count, i) for i in range(ends)]),
            ],
            axis=dim,
        )
    return cells


def gelu_exact(value):
    return jax.nn.gelu(value, approximate=False)


def gelu_back(value, grad_value):
    _, pull = jax.vjp(gelu_exact, value)
    return pull(grad_value)[0]


def gram_dot(left, right):
    return lax.dot_general(
        left, right, (((0,), (0,)), ((), ())), preferred_element_type=jnp.float32
    )


def times_t(left, right):
    return lax.dot_general(
        left, right, (((1,), (1,)), ((), ())), preferred_element_type=jnp.float32
    )


def fetch_weights(shards):
    return (
        lax.all_gather(shards[0], "seq", axis=0, tiled=True),
        lax.all_gather(shards[1], "seq", axis=2, tiled=True),
        lax.all_gather(shards[2], "seq", axis=0, tiled=True),
        lax.all_gather(shards[3], "seq", axis=1, tiled=True),
        lax.all_gather(shards[4], "seq", axis=0, tiled=True),
        lax.all_gather(shards[5], "seq", axis=0, tiled=True),
        lax.all_gather(shards[6], "seq", axis=0, tiled=True),
        lax.all_gather(shards[7], "seq", axis=1, tiled=True),
        lax.all_gather(shards[8], "seq", axis=0, tiled=True),
        lax.all_gather(shards[9], "seq", axis=0, tiled=True),
        lax.all_gather(shards[10], "seq", axis=0, tiled=True),
        lax.all_gather(shards[11], "seq", axis=1, tiled=True),
    )


def spread_grads(gradients):
    return (
        lax.psum_scatter(
            gradients[0].astype(jnp.bfloat16), "seq", scatter_dimension=0, tiled=True
        ).astype(jnp.float32),
        lax.psum_scatter(
            gradients[1].astype(jnp.bfloat16), "seq", scatter_dimension=2, tiled=True
        ).astype(jnp.float32),
        lax.psum_scatter(
            gradients[2].astype(jnp.bfloat16), "seq", scatter_dimension=0, tiled=True
        ).astype(jnp.float32),
        lax.psum_scatter(
            gradients[3].astype(jnp.bfloat16), "seq", scatter_dimension=1, tiled=True
        ).astype(jnp.float32),
        lax.psum_scatter(
            gradients[4].astype(jnp.bfloat16), "seq", scatter_dimension=0, tiled=True
        ).astype(jnp.float32),
        lax.psum_scatter(
            gradients[5].astype(jnp.bfloat16), "seq", scatter_dimension=0, tiled=True
        ).astype(jnp.float32),
        lax.psum_scatter(
            gradients[6].astype(jnp.bfloat16), "seq", scatter_dimension=0, tiled=True
        ).astype(jnp.float32),
        lax.psum_scatter(
            gradients[7].astype(jnp.bfloat16), "seq", scatter_dimension=1, tiled=True
        ).astype(jnp.float32),
        lax.psum_scatter(
            gradients[8].astype(jnp.bfloat16), "seq", scatter_dimension=0, tiled=True
        ).astype(jnp.float32),
        lax.psum_scatter(
            gradients[9].astype(jnp.bfloat16), "seq", scatter_dimension=0, tiled=True
        ).astype(jnp.float32),
        lax.psum_scatter(
            gradients[10].astype(jnp.bfloat16), "seq", scatter_dimension=0, tiled=True
        ).astype(jnp.float32),
        lax.psum_scatter(
            gradients[11].astype(jnp.bfloat16), "seq", scatter_dimension=1, tiled=True
        ).astype(jnp.float32),
    )


def gather_rows(value):
    return lax.all_gather(value, "cond", axis=1, tiled=True)


def share_rows(value):
    return lax.psum_scatter(value, "cond", scatter_dimension=1, tiled=True)


def moments(first_part, second_part):
    return lax.psum((first_part, second_part), "cond")


def norm_forward(stream, full_width):
    tot_sum, tot_sq = moments(jnp.sum(stream, axis=1), jnp.sum(stream * stream, axis=1))
    mean_row = tot_sum / full_width
    var_row = tot_sq / full_width - mean_row * mean_row
    rstd_row = lax.rsqrt(var_row + EPSILON)
    return ((stream - mean_row[:, None]) * rstd_row[:, None], rstd_row)


def norm_backward(normed, rstd_row, gain, grad_norm, full_width):
    scaled = grad_norm * gain
    tot_first, tot_second = moments(jnp.sum(scaled, axis=1), jnp.sum(scaled * normed, axis=1))
    grad_stream = rstd_row[:, None] * (
        scaled - tot_first[:, None] / full_width - normed * tot_second[:, None] / full_width
    )
    return (grad_stream, jnp.sum(grad_norm * normed, axis=0), jnp.sum(grad_norm, axis=0))


def attend_scores(query_part, key_part, allowed, score_scale):
    scores = (
        jnp.einsum("bqhd,bkhd->bhqk", query_part, key_part, preferred_element_type=jnp.float32)
        * score_scale
    )
    return jnp.where(allowed, scores, NEG_FILL)


def one_micro(inputs, coarse, segments, cotangent, full):
    (
        embed_table,
        conv_weight,
        res_weight,
        up_weight,
        gain_one,
        shift_one,
        qkv_weight,
        out_weight,
        gain_two,
        shift_two,
        in_weight,
        down_weight,
    ) = full
    tokens, quarter = inputs.shape
    model_width = quarter * lax.axis_size("cond")
    coarse_length = coarse.shape[0]
    dilation_step = CONV_DILATION
    table_rows = embed_table.shape[0]
    onehot = (coarse[:, None] == jnp.arange(table_rows, dtype=jnp.int32)[None, :]).astype(
        jnp.bfloat16
    )
    embed = jnp.dot(onehot, embed_table, preferred_element_type=jnp.float32)
    coarse_activation_rows = gelu_exact(embed).astype(jnp.bfloat16)
    padded_input = extended(coarse_activation_rows, (("seq", 0),), dilation_step)
    kernel_tap_rows = jnp.concatenate(
        [
            padded_input[kernel_tap * dilation_step : kernel_tap * dilation_step + coarse_length]
            for kernel_tap in range(3)
        ],
        axis=1,
    )
    conv_flat = conv_weight.reshape(3 * quarter, model_width)
    conv_out = lax.psum(
        jnp.dot(kernel_tap_rows, conv_flat, preferred_element_type=jnp.float32), "cond"
    )
    mixed_act = gelu_exact(conv_out).astype(jnp.bfloat16)
    res_out = jnp.dot(mixed_act, res_weight, preferred_element_type=jnp.float32)
    hidden_cond = (embed + res_out).astype(jnp.bfloat16)
    up_terms = jnp.dot(hidden_cond, up_weight, preferred_element_type=jnp.float32).reshape(
        tokens, model_width
    )
    stream_zero = inputs.astype(jnp.float32) + share_rows(up_terms)
    gain_first = gain_one.astype(jnp.float32)
    gain_second = gain_two.astype(jnp.float32)
    normed_one, rstd_one = norm_forward(stream_zero, model_width)
    norm_one = gather_rows(
        (normed_one * gain_first + shift_one.astype(jnp.float32)).astype(jnp.bfloat16)
    )
    qkv_all = jnp.einsum(
        "td,dje->tje", norm_one, qkv_weight, preferred_element_type=jnp.float32
    ).astype(jnp.bfloat16)
    local_width = qkv_all.shape[2]
    head_count = local_width // HEAD
    row_count = tokens // ROW
    block_shape = (row_count, ROW, head_count, HEAD)
    query_part = qkv_all[:, 0].reshape(block_shape)
    key_part = qkv_all[:, 1].reshape(block_shape)
    value_part = qkv_all[:, 2].reshape(block_shape)
    seg_rows = segments.reshape(row_count, ROW)
    places = jnp.arange(ROW)
    allowed = (
        (seg_rows[:, :, None] == seg_rows[:, None, :]) & (places[:, None] >= places[None, :])[None]
    )[:, None]
    score_scale = 1.0 / math.sqrt(HEAD)
    scores = attend_scores(query_part, key_part, allowed, score_scale)
    row_max = jnp.max(scores, axis=-1, keepdims=True)
    row_exp = jnp.exp(scores - row_max)
    row_total = jnp.sum(row_exp, axis=-1, keepdims=True)
    log_total = row_max + jnp.log(row_total)
    probs_low = (row_exp / row_total).astype(jnp.bfloat16)
    context = jnp.einsum(
        "bhqk,bkhd->bqhd", probs_low, value_part, preferred_element_type=jnp.float32
    )
    context = context.astype(jnp.bfloat16).reshape(tokens, local_width)
    stream_one = stream_zero + share_rows(
        jnp.dot(context, out_weight, preferred_element_type=jnp.float32)
    )
    normed_two, rstd_two = norm_forward(stream_one, model_width)
    norm_two = gather_rows(
        (normed_two * gain_second + shift_two.astype(jnp.float32)).astype(jnp.bfloat16)
    )
    mlp_pre = jnp.dot(norm_two, in_weight, preferred_element_type=jnp.float32)
    mlp_act = gelu_exact(mlp_pre).astype(jnp.bfloat16)
    stream_two = stream_one + share_rows(
        jnp.dot(mlp_act, down_weight, preferred_element_type=jnp.float32)
    )
    result = stream_two.astype(jnp.bfloat16)
    cot_whole = gather_rows(cotangent)
    grad_down = gram_dot(mlp_act, cot_whole)
    grad_pre = gelu_back(mlp_pre, times_t(cot_whole, down_weight)).astype(jnp.bfloat16)
    grad_in = gram_dot(norm_two, grad_pre)
    grad_norm_two = share_rows(times_t(grad_pre, in_weight))
    back_two, grad_gain_two, grad_shift_two = norm_backward(
        normed_two, rstd_two, gain_second, grad_norm_two, model_width
    )
    grad_stream_one = cotangent.astype(jnp.float32) + back_two
    grad_att = gather_rows(grad_stream_one.astype(jnp.bfloat16))
    grad_out = gram_dot(context, grad_att)
    grad_context = times_t(grad_att, out_weight).astype(jnp.bfloat16).reshape(block_shape)
    attn_probs = jnp.exp(attend_scores(query_part, key_part, allowed, score_scale) - log_total)
    probs_low = attn_probs.astype(jnp.bfloat16)
    grad_probs = jnp.einsum(
        "bqhd,bkhd->bhqk", grad_context, value_part, preferred_element_type=jnp.float32
    )
    inner_row = jnp.sum(attn_probs * grad_probs, axis=-1, keepdims=True)
    grad_scores = (attn_probs * (grad_probs - inner_row)).astype(jnp.bfloat16)
    grad_query = (
        jnp.einsum("bhqk,bkhd->bqhd", grad_scores, key_part, preferred_element_type=jnp.float32)
        * score_scale
    ).astype(jnp.bfloat16)
    grad_keys = (
        jnp.einsum("bhqk,bqhd->bkhd", grad_scores, query_part, preferred_element_type=jnp.float32)
        * score_scale
    ).astype(jnp.bfloat16)
    grad_values = jnp.einsum(
        "bhqk,bqhd->bkhd", probs_low, grad_context, preferred_element_type=jnp.float32
    ).astype(jnp.bfloat16)
    grad_rows = jnp.stack(
        [
            grad_query.reshape(tokens, local_width),
            grad_keys.reshape(tokens, local_width),
            grad_values.reshape(tokens, local_width),
        ],
        axis=1,
    )
    grad_qkv = jnp.einsum("td,tje->dje", norm_one, grad_rows, preferred_element_type=jnp.float32)
    grad_norm_one = share_rows(
        jnp.einsum("tje,dje->td", grad_rows, qkv_weight, preferred_element_type=jnp.float32)
    )
    back_one, grad_gain_one, grad_shift_one = norm_backward(
        normed_one, rstd_one, gain_first, grad_norm_one, model_width
    )
    input_grad = (grad_stream_one + back_one).astype(jnp.bfloat16)
    grad_up_rows = gather_rows(input_grad).reshape(coarse_length, 4 * model_width)
    grad_up = gram_dot(hidden_cond, grad_up_rows)
    grad_hidden = times_t(grad_up_rows, up_weight)
    grad_res_low = grad_hidden.astype(jnp.bfloat16)
    grad_res = gram_dot(mixed_act, grad_res_low)
    grad_mixed = lax.psum(times_t(grad_res_low, res_weight).astype(jnp.bfloat16), "cond").astype(
        jnp.float32
    )
    grad_conv_low = gelu_back(conv_out, grad_mixed).astype(jnp.bfloat16)
    grad_conv = gram_dot(kernel_tap_rows, grad_conv_low).reshape(3, quarter, model_width)
    grad_taps = times_t(grad_conv_low, conv_flat)
    grad_padded = jnp.pad(grad_taps[:, 0:quarter], ((0, 2 * dilation_step), (0, 0)))
    grad_padded = grad_padded + jnp.pad(
        grad_taps[:, quarter : 2 * quarter], ((dilation_step, dilation_step), (0, 0))
    )
    grad_padded = grad_padded + jnp.pad(
        grad_taps[:, 2 * quarter :], ((2 * dilation_step, 0), (0, 0))
    )
    rim_grads = jnp.concatenate(
        [grad_padded[:dilation_step], grad_padded[coarse_length + dilation_step :]], axis=0
    )
    rim_values = extended(rim_grads.astype(jnp.bfloat16), (("seq", 0),), dilation_step).astype(
        rim_grads.dtype
    )
    grad_act = grad_padded[dilation_step : dilation_step + coarse_length]
    grad_act = grad_act + jnp.pad(
        rim_values[:dilation_step], ((0, coarse_length - dilation_step), (0, 0))
    )
    grad_act = grad_act + jnp.pad(
        rim_values[3 * dilation_step :], ((coarse_length - dilation_step, 0), (0, 0))
    )
    grad_embed = (grad_hidden + gelu_back(embed, grad_act)).astype(jnp.bfloat16)
    grad_table = gram_dot(onehot, grad_embed)
    gradients = (
        grad_table,
        grad_conv,
        grad_res,
        grad_up,
        grad_gain_one,
        grad_shift_one,
        grad_qkv,
        grad_out,
        grad_gain_two,
        grad_shift_two,
        grad_in,
        grad_down,
    )
    return (result, input_grad, gradients)


def on_device(
    inputs,
    coarse_ids,
    segment_ids,
    cotangent,
    embed_table,
    conv_weight,
    res_weight,
    up_weight,
    gain_one,
    shift_one,
    qkv_weight,
    out_weight,
    gain_two,
    shift_two,
    in_weight,
    down_weight,
):
    shards = (
        embed_table,
        conv_weight,
        res_weight,
        up_weight,
        gain_one,
        shift_one,
        qkv_weight,
        out_weight,
        gain_two,
        shift_two,
        in_weight,
        down_weight,
    )
    outputs = []
    in_grads = []
    summed = None
    for index in range(inputs.shape[0]):
        full = fetch_weights(shards)
        result, input_grad, gradients = one_micro(
            inputs[index], coarse_ids[index], segment_ids[index], cotangent[index], full
        )
        outputs.append(result)
        in_grads.append(input_grad)
        shares = spread_grads(gradients)
        summed = shares if summed is None else jax.tree.map(jnp.add, summed, shares)
    return (jnp.stack(outputs), jnp.stack(in_grads)) + tuple(summed)


def solution(mesh):
    return jax.shard_map(
        on_device,
        mesh=mesh,
        in_specs=(
            P(None, "seq", "cond"),
            P(None, "seq"),
            P(None, "seq"),
            P(None, "seq", "cond"),
            P("seq", "cond"),
            P(None, "cond", "seq"),
            P("seq", "cond"),
            P("cond", "seq"),
            P(("cond", "seq")),
            P(("cond", "seq")),
            P("seq", None, "cond"),
            P("cond", "seq"),
            P(("cond", "seq")),
            P(("cond", "seq")),
            P("seq", "cond"),
            P("cond", "seq"),
        ),
        out_specs=(
            P(None, "seq", "cond"),
            P(None, "seq", "cond"),
            P("seq", "cond"),
            P(None, "cond", "seq"),
            P("seq", "cond"),
            P("cond", "seq"),
            P(("cond", "seq")),
            P(("cond", "seq")),
            P("seq", None, "cond"),
            P("cond", "seq"),
            P(("cond", "seq")),
            P(("cond", "seq")),
            P("seq", "cond"),
            P("cond", "seq"),
        ),
        check_vma=False,
    )
```

profile of v0, /device:TPU:0, one launch (start us, length us, event | category | flops | bytes accessed | tf_op | source)
XLA Modules:
  0.0 3656.3 jit_solution(12000477826808269472)
XLA Ops:
  9.6 43.4 %all-gather.31.cloned.1.call-done = bf16[2048,256]{1,0:T(8,128)(2,1)} async-done(((bf16[256,256]{1,0:T(8,128)(2,1)}), bf16[2048,256]{1,0:T(8,128)(2,1)}) %all-gather.31.cloned.1.call-update) | async-done | bytes 1048592 | tf_op jit(solution)/shard_map/all_gather | solution.py:54
  77.3 22.3 all-gather.33.cloned.1.call-done
  111.0 31.5 all_gather.66
  142.5 19.0 all-reduce.51.cloned.1.call-done
  166.6 48.3 %all-gather.35.cloned.1.call-done = bf16[256,4096]{1,0:T(8,128)(2,1)} async-done(((bf16[256,512]{1,0:T(8,128)(2,1)}), bf16[256,4096]{1,0:T(8,128)(2,1)}) %all-gather.35.cloned.1.call-update) | async-done | bytes 2097168 | tf_op jit(solution)/shard_map/all_gather | solution.py:57
  246.0 18.9 all-reduce.46
  265.0 17.2 reduce-scatter.83.cloned.1.call-done
  282.2 34.2 reduce-scatter.89.cloned.1.call-done
  316.4 34.0 reduce-scatter.95.cloned.1.call-done
  366.3 29.8 all_gather.140
  402.3 17.5 all-gather.55.cloned.1.call-done
  491.8 19.1 reduce-scatter.97.cloned.1.call-done
  512.8 31.9 reduce-scatter.91.cloned.1.call-done
  546.0 32.8 reduce-scatter.85.cloned.1.call-done
  580.0 32.6 reduce-scatter.79.cloned.1.call-done
  633.8 30.3 all-gather.43.cloned.1.call-done
  664.1 17.6 all-gather.57.cloned.1.call-done
  700.0 53.4 %all-gather.45.cloned.1.call-done = bf16[1024,1024]{1,0:T(8,128)(2,1)} async-done(((bf16[1024,128]{1,0:T(8,128)(2,1)}), bf16[1024,1024]{1,0:T(8,128)(2,1)}) %all-gather.45.cloned.1.call-update) | async-done | bytes 2097168 | tf_op jit(solution)/shard_map/all_gather | solution.py:65
  898.1 34.0 reduce-scatter.109.cloned.1.call-done
  932.1 34.0 reduce-scatter.105.cloned.1.call-done
  966.1 34.0 reduce-scatter.101.cloned.1.call-done
  1013.4 20.9 reduce-scatter.99.cloned.1.call-done
  1034.3 33.8 reduce-scatter.81.cloned.1.call-done
  1071.9 30.4 reduce-scatter.93.cloned.1.call-done
  1102.3 34.0 reduce-scatter.87.cloned.1.call-done
  1140.2 15.0 all-gather.65.cloned.1.call-done
  1222.2 23.0 reduce-scatter.115.cloned.1.call-done
  1245.2 34.0 reduce-scatter.103.cloned.1.call-done
  1279.2 34.2 reduce-scatter.111.cloned.1.call-done
  1313.4 33.8 reduce-scatter.107.cloned.1.call-done
  1384.0 15.9 all-gather.71.cloned.1.call-done
  1402.4 16.4 all-gather.67.cloned.1.call-done
  1601.5 19.8 reduce-scatter.177.cloned.1.call-done
  1622.4 69.0 %reduce-scatter.175.cloned.1.call-done = bf16[128,1024]{1,0:T(8,128)(2,1)} async-done(((bf16[1024,1024]{1,0:T(8,128)(2,1)}), bf16[128,1024]{1,0:T(8,128)(2,1)}) %reduce-scatter.175.cloned.1.call-update) | async-done | bytes 262160
  1692.5 69.1 %reduce-scatter.173.cloned.1.call-done = bf16[128,1024]{1,0:T(8,128)(2,1)} async-done(((bf16[1024,1024]{1,0:T(8,128)(2,1)}), bf16[128,1024]{1,0:T(8,128)(2,1)}) %reduce-scatter.173.cloned.1.call-update) | async-done | bytes 262160
  1764.9 66.7 %reduce-scatter.155.cloned.1.call-done = bf16[128,1024]{1,0:T(8,128)(2,1)} async-done(((bf16[1024,1024]{1,0:T(8,128)(2,1)}), bf16[128,1024]{1,0:T(8,128)(2,1)}) %reduce-scatter.155.cloned.1.call-update) | async-done | bytes 262160 | tf_op jit(solution)/shard_map/reduce_scatter | solution.py:101
  1831.7 70.3 %reduce-scatter.153.cloned.1.call-done = bf16[128,1024]{1,0:T(8,128)(2,1)} async-done(((bf16[1024,1024]{1,0:T(8,128)(2,1)}), bf16[128,1024]{1,0:T(8,128)(2,1)}) %reduce-scatter.153.cloned.1.call-update) | async-done | bytes 262160 | tf_op jit(solution)/shard_map/reduce_scatter | solution.py:101
  1902.0 70.2 %reduce-scatter.151.cloned.1.call-done = bf16[128,1024]{1,0:T(8,128)(2,1)} async-done(((bf16[1024,1024]{1,0:T(8,128)(2,1)}), bf16[128,1024]{1,0:T(8,128)(2,1)}) %reduce-scatter.151.cloned.1.call-update) | async-done | bytes 262160 | tf_op jit(solution)/shard_map/reduce_scatter | solution.py:101
  1972.2 70.2 %reduce-scatter.149.cloned.1.call-done = bf16[128,1024]{1,0:T(8,128)(2,1)} async-done(((bf16[1024,1024]{1,0:T(8,128)(2,1)}), bf16[128,1024]{1,0:T(8,128)(2,1)}) %reduce-scatter.149.cloned.1.call-update) | async-done | bytes 262160 | tf_op jit(solution)/shard_map/reduce_scatter | solution.py:101
  2044.6 62.7 %reduce-scatter.171.cloned.1.call-done = bf16[128,256]{1,0:T(8,128)(2,1)} async-done(((bf16[1024,256]{1,0:T(8,128)(2,1)}), bf16[128,256]{1,0:T(8,128)(2,1)}) %reduce-scatter.171.cloned.1.call-update) | async-done | bytes 65552
  2108.2 63.6 %reduce-scatter.165.cloned.1.call-done = bf16[128,256]{1,0:T(8,128)(2,1)} async-done(((bf16[1024,256]{1,0:T(8,128)(2,1)}), bf16[128,256]{1,0:T(8,128)(2,1)}) %reduce-scatter.165.cloned.1.call-update) | async-done | bytes 65552
  2172.8 63.1 %reduce-scatter.169.cloned.1.call-done = bf16[128,256]{1,0:T(8,128)(2,1)} async-done(((bf16[1024,256]{1,0:T(8,128)(2,1)}), bf16[128,256]{1,0:T(8,128)(2,1)}) %reduce-scatter.169.cloned.1.call-update) | async-done | bytes 65552
  2236.8 63.8 %reduce-scatter.167.cloned.1.call-done = bf16[128,256]{1,0:T(8,128)(2,1)} async-done(((bf16[1024,256]{1,0:T(8,128)(2,1)}), bf16[128,256]{1,0:T(8,128)(2,1)}) %reduce-scatter.167.cloned.1.call-update) | async-done | bytes 65552
  2302.3 66.3 %reduce-scatter.145.cloned.1.call-done = bf16[128,3,256]{2,0,1:T(8,128)(2,1)} async-done(((bf16[1024,3,256]{2,0,1:T(8,128)(2,1)}), bf16[128,3,256]{2,0,1:T(8,128)(2,1)}) %reduce-scatter.145.cloned.1.call-update) | async-done | bytes 196624 | tf_op jit(solution)/shard_map/reduce_scatter | solution.py:89
  2368.6 68.4 %reduce-scatter.143.cloned.1.call-done = bf16[128,3,256]{2,0,1:T(8,128)(2,1)} async-done(((bf16[1024,3,256]{2,0,1:T(8,128)(2,1)}), bf16[128,3,256]{2,0,1:T(8,128)(2,1)}) %reduce-scatter.143.cloned.1.call-update) | async-done | bytes 196624 | tf_op jit(solution)/shard_map/reduce_scatter | solution.py:89
  2437.0 67.8 %reduce-scatter.141.cloned.1.call-done = bf16[128,3,256]{2,0,1:T(8,128)(2,1)} async-done(((bf16[1024,3,256]{2,0,1:T(8,128)(2,1)}), bf16[128,3,256]{2,0,1:T(8,128)(2,1)}) %reduce-scatter.141.cloned.1.call-update) | async-done | bytes 196624 | tf_op jit(solution)/shard_map/reduce_scatter | solution.py:89
  2504.8 68.2 %reduce-scatter.147.cloned.1.call-done = bf16[128,3,256]{2,0,1:T(8,128)(2,1)} async-done(((bf16[1024,3,256]{2,0,1:T(8,128)(2,1)}), bf16[128,3,256]{2,0,1:T(8,128)(2,1)}) %reduce-scatter.147.cloned.1.call-update) | async-done | bytes 196624 | tf_op jit(solution)/shard_map/reduce_scatter | solution.py:89
  2575.2 19.8 all-reduce.45
  2598.5 38.8 %reduce-scatter.127.cloned.1.call-done = bf16[128,256]{1,0:T(8,128)(2,1)} async-done(((bf16[1024,256]{1,0:T(8,128)(2,1)}), bf16[128,256]{1,0:T(8,128)(2,1)}) %reduce-scatter.127.cloned.1.call-update) | async-done | bytes 65552 | tf_op jit(solution)/shard_map/reduce_scatter | solution.py:77
  2637.3 64.5 %reduce-scatter.129.cloned.1.call-done = bf16[128,256]{1,0:T(8,128)(2,1)} async-done(((bf16[1024,256]{1,0:T(8,128)(2,1)}), bf16[128,256]{1,0:T(8,128)(2,1)}) %reduce-scatter.129.cloned.1.call-update) | async-done | bytes 65552 | tf_op jit(solution)/shard_map/reduce_scatter | solution.py:77
  2701.8 64.2 %reduce-scatter.125.cloned.1.call-done = bf16[128,256]{1,0:T(8,128)(2,1)} async-done(((bf16[1024,256]{1,0:T(8,128)(2,1)}), bf16[128,256]{1,0:T(8,128)(2,1)}) %reduce-scatter.125.cloned.1.call-update) | async-done | bytes 65552 | tf_op jit(solution)/shard_map/reduce_scatter | solution.py:77
  2765.9 64.7 %reduce-scatter.131.cloned.1.call-done = bf16[128,256]{1,0:T(8,128)(2,1)} async-done(((bf16[1024,256]{1,0:T(8,128)(2,1)}), bf16[128,256]{1,0:T(8,128)(2,1)}) %reduce-scatter.131.cloned.1.call-update) | async-done | bytes 65552 | tf_op jit(solution)/shard_map/reduce_scatter | solution.py:77
  2832.3 64.2 %reduce-scatter.117.cloned.1.call-done = bf16[256,256]{1,0:T(8,128)(2,1)} async-done(((bf16[2048,256]{1,0:T(8,128)(2,1)}), bf16[256,256]{1,0:T(8,128)(2,1)}) %reduce-scatter.117.cloned.1.call-update) | async-done | bytes 131088 | tf_op jit(solution)/shard_map/reduce_scatter | solution.py:71
  2896.5 66.2 %reduce-scatter.119.cloned.1.call-done = bf16[256,256]{1,0:T(8,128)(2,1)} async-done(((bf16[2048,256]{1,0:T(8,128)(2,1)}), bf16[256,256]{1,0:T(8,128)(2,1)}) %reduce-scatter.119.cloned.1.call-update) | async-done | bytes 131088 | tf_op jit(solution)/shard_map/reduce_scatter | solution.py:71
  2962.6 65.8 %reduce-scatter.121.cloned.1.call-done = bf16[256,256]{1,0:T(8,128)(2,1)} async-done(((bf16[2048,256]{1,0:T(8,128)(2,1)}), bf16[256,256]{1,0:T(8,128)(2,1)}) %reduce-scatter.121.cloned.1.call-update) | async-done | bytes 131088 | tf_op jit(solution)/shard_map/reduce_scatter | solution.py:71
  3028.4 66.0 %reduce-scatter.123.cloned.1.call-done = bf16[256,256]{1,0:T(8,128)(2,1)} async-done(((bf16[2048,256]{1,0:T(8,128)(2,1)}), bf16[256,256]{1,0:T(8,128)(2,1)}) %reduce-scatter.123.cloned.1.call-update) | async-done | bytes 131088 | tf_op jit(solution)/shard_map/reduce_scatter | solution.py:71
  3096.3 65.2 %reduce-scatter.157.cloned.1.call-done = bf16[128,768]{1,0:T(8,128)(2,1)} async-done(((bf16[1024,768]{1,0:T(8,128)(2,1)}), bf16[128,768]{1,0:T(8,128)(2,1)}) %reduce-scatter.157.cloned.1.call-update) | async-done | bytes 196624
  3162.7 66.2 %reduce-scatter.159.cloned.1.call-done = bf16[128,768]{1,0:T(8,128)(2,1)} async-done(((bf16[1024,768]{1,0:T(8,128)(2,1)}), bf16[128,768]{1,0:T(8,128)(2,1)}) %reduce-scatter.159.cloned.1.call-update) | async-done | bytes 196624
  3230.2 65.9 %reduce-scatter.161.cloned.1.call-done = bf16[128,768]{1,0:T(8,128)(2,1)} async-done(((bf16[1024,768]{1,0:T(8,128)(2,1)}), bf16[128,768]{1,0:T(8,128)(2,1)}) %reduce-scatter.161.cloned.1.call-update) | async-done | bytes 196624
  3297.3 66.3 %reduce-scatter.163.cloned.1.call-done = bf16[128,768]{1,0:T(8,128)(2,1)} async-done(((bf16[1024,768]{1,0:T(8,128)(2,1)}), bf16[128,768]{1,0:T(8,128)(2,1)}) %reduce-scatter.163.cloned.1.call-update) | async-done | bytes 196624
  3365.7 68.7 %reduce-scatter.135.cloned.1.call-done = bf16[256,512]{1,0:T(8,128)(2,1)} async-done(((bf16[256,4096]{1,0:T(8,128)(2,1)}), bf16[256,512]{1,0:T(8,128)(2,1)}) %reduce-scatter.135.cloned.1.call-update) | async-done | bytes 262160 | tf_op jit(solution)/shard_map/reduce_scatter | solution.py:80
  3434.4 70.8 %reduce-scatter.137.cloned.1.call-done = bf16[256,512]{1,0:T(8,128)(2,1)} async-done(((bf16[256,4096]{1,0:T(8,128)(2,1)}), bf16[256,512]{1,0:T(8,128)(2,1)}) %reduce-scatter.137.cloned.1.call-update) | async-done | bytes 262160 | tf_op jit(solution)/shard_map/reduce_scatter | solution.py:80
  3505.2 71.0 %reduce-scatter.133.cloned.1.call-done = bf16[256,512]{1,0:T(8,128)(2,1)} async-done(((bf16[256,4096]{1,0:T(8,128)(2,1)}), bf16[256,512]{1,0:T(8,128)(2,1)}) %reduce-scatter.133.cloned.1.call-update) | async-done | bytes 262160 | tf_op jit(solution)/shard_map/reduce_scatter | solution.py:80
  3576.2 70.8 %reduce-scatter.139.cloned.1.call-done = bf16[256,512]{1,0:T(8,128)(2,1)} async-done(((bf16[256,4096]{1,0:T(8,128)(2,1)}), bf16[256,512]{1,0:T(8,128)(2,1)}) %reduce-scatter.139.cloned.1.call-update) | async-done | bytes 262160 | tf_op jit(solution)/shard_map/reduce_scatter | solution.py:80
  (987 shorter events, 690.2 us)
Async XLA Ops:
  8.7 152.9 %all-reduce.51.cloned.1.call-start = ((), (), s32[]{:S(2)}) async-start(), calls=%async_computation.130 | async-start | bytes 4194304 | tf_op jit(solution)/shard_map/psum | solution.py:181
  111.0 154.0 %reduce-scatter.77.cloned.1.call-start = ((), (), s32[]{:S(2)}) async-start(), calls=%async_computation.55 | async-start | bytes 2621440 | tf_op jit(solution)/shard_map/reduce_scatter | solution.py:115
  237.2 113.1 %reduce-scatter.95.cloned.1.call-start = ((), (), s32[]{:S(2)}) async-start(), calls=%async_computation.73 | async-start | bytes 2621440 | tf_op jit(solution)/shard_map/reduce_scatter | solution.py:115
  242.9 159.4 %all-gather.39.cloned.1.call-start = ((), (), s32[]{:S(2)}) async-start(), calls=%async_computation.57 | async-start | bytes 1769472 | tf_op jit(solution)/shard_map/all_gather | solution.py:60
  243.7 176.1 %all-gather.55.cloned.1.call-start = ((), (), s32[]{:S(2)}) async-start(), calls=%async_computation.74 | async-start | bytes 1310720 | tf_op jit(solution)/shard_map/all_gather | solution.py:111
  365.9 111.0 %all-gather.37.cloned.1.call-start = ((), (), s32[]{:S(2)}) async-start(), calls=%async_computation.56 | async-start | bytes 1310720 | tf_op jit(solution)/shard_map/all_gather | solution.py:111
  397.2 113.7 %reduce-scatter.97.cloned.1.call-start = ((), (), s32[]{:S(2)}) async-start(), calls=%async_computation.75 | async-start | bytes 2621440 | tf_op jit(solution)/shard_map/reduce_scatter | solution.py:115
  455.1 123.7 %reduce-scatter.85.cloned.1.call-start = ((), (), s32[]{:S(2)}) async-start(), calls=%async_computation.65 | async-start | bytes 2621440 | tf_op jit(solution)/shard_map/reduce_scatter | solution.py:115
  474.1 138.5 %reduce-scatter.79.cloned.1.call-start = ((), (), s32[]{:S(2)}) async-start(), calls=%async_computation.58 | async-start | bytes 2621440 | tf_op jit(solution)/shard_map/reduce_scatter | solution.py:115
  491.2 172.9 %all-gather.43.cloned.1.call-start = ((), (), s32[]{:S(2)}) async-start(), calls=%async_computation.60 | async-start | bytes 2359296 | tf_op jit(solution)/shard_map/all_gather | solution.py:64
  491.8 189.9 %all-gather.57.cloned.1.call-start = ((), (), s32[]{:S(2)}) async-start(), calls=%async_computation.76 | async-start | bytes 1310720 | tf_op jit(solution)/shard_map/all_gather | solution.py:111
  628.9 124.5 %all-gather.45.cloned.1.call-start = ((), (), s32[]{:S(2)}) async-start(), calls=%async_computation.61 | async-start | bytes 2359296 | tf_op jit(solution)/shard_map/all_gather | solution.py:65
  629.6 141.0 %all-gather.53.cloned.1.call-start = ((), (), s32[]{:S(2)}) async-start(), calls=%async_computation.71 | async-start | bytes 1310720 | tf_op jit(solution)/shard_map/all_gather | solution.py:111
  630.4 158.8 %all-gather.79.cloned.1.call-start = ((), (), s32[]{:S(2)}) async-start(), calls=%async_computation.116 | async-start | bytes 1310720 | tf_op jit(solution)/shard_map/all_gather | solution.py:111
  631.1 177.0 %all-gather.49.cloned.1.call-start = ((), (), s32[]{:S(2)}) async-start(), calls=%async_computation.66 | async-start | bytes 1310720 | tf_op jit(solution)/shard_map/all_gather | solution.py:111
  631.7 194.9 %all-gather.77.cloned.1.call-start = ((), (), s32[]{:S(2)}) async-start(), calls=%async_computation.115 | async-start | bytes 1310720 | tf_op jit(solution)/shard_map/all_gather | solution.py:111
  632.4 213.1 %all-gather.41.cloned.1.call-start = ((), (), s32[]{:S(2)}) async-start(), calls=%async_computation.59 | async-start | bytes 1310720 | tf_op jit(solution)/shard_map/all_gather | solution.py:111
  633.0 230.9 %all-gather.75.cloned.1.call-start = ((), (), s32[]{:S(2)}) async-start(), calls=%async_computation.114 | async-start | bytes 1310720 | tf_op jit(solution)/shard_map/all_gather | solution.py:111
  633.6 264.5 %reduce-scatter.113.cloned.1.call-start = ((), (), s32[]{:S(2)}) async-start(), calls=%async_computation.87 | async-start | bytes 2621440 | tf_op jit(solution)/shard_map/reduce_scatter | solution.py:115
  762.1 170.0 %reduce-scatter.109.cloned.1.call-start = ((), (), s32[]{:S(2)}) async-start(), calls=%async_computation.84 | async-start | bytes 2621440 | tf_op jit(solution)/shard_map/reduce_scatter | solution.py:115
  798.0 168.1 %reduce-scatter.105.cloned.1.call-start = ((), (), s32[]{:S(2)}) async-start(), calls=%async_computation.81 | async-start | bytes 2621440 | tf_op jit(solution)/shard_map/reduce_scatter | solution.py:115
  835.4 164.7 %reduce-scatter.101.cloned.1.call-start = ((), (), s32[]{:S(2)}) async-start(), calls=%async_computation.78 | async-start | bytes 2621440 | tf_op jit(solution)/shard_map/reduce_scatter | solution.py:115
  872.6 161.7 %reduce-scatter.99.cloned.1.call-start = ((), (), s32[]{:S(2)}) async-start(), calls=%async_computation.77 | async-start | bytes 2621440 | tf_op jit(solution)/shard_map/reduce_scatter | solution.py:115
  877.5 190.6 %reduce-scatter.81.cloned.1.call-start = ((), (), s32[]{:S(2)}) async-start(), calls=%async_computation.62 | async-start | bytes 2621440 | tf_op jit(solution)/shard_map/reduce_scatter | solution.py:115
  882.5 219.8 %reduce-scatter.93.cloned.1.call-start = ((), (), s32[]{:S(2)}) async-start(), calls=%async_computation.72 | async-start | bytes 2621440 | tf_op jit(solution)/shard_map/reduce_scatter | solution.py:115
  887.5 248.8 %reduce-scatter.87.cloned.1.call-start = ((), (), s32[]{:S(2)}) async-start(), calls=%async_computation.67 | async-start | bytes 2621440 | tf_op jit(solution)/shard_map/reduce_scatter | solution.py:115
  892.0 263.2 %all-gather.65.cloned.1.call-start = ((), (), s32[]{:S(2)}) async-start(), calls=%async_computation.88 | async-start | bytes 1310720 | tf_op jit(solution)/shard_map/all_gather | solution.py:111
  1071.8 120.8 %all-gather.63.cloned.1.call-start = ((), (), s32[]{:S(2)}) async-start(), calls=%async_computation.85 | async-start | bytes 1310720 | tf_op jit(solution)/shard_map/all_gather | solution.py:111
  1191.4 121.9 %reduce-scatter.111.cloned.1.call-start = ((), (), s32[]{:S(2)}) async-start(), calls=%async_computation.86 | async-start | bytes 2621440 | tf_op jit(solution)/shard_map/reduce_scatter | solution.py:115
  1206.4 140.8 %reduce-scatter.107.cloned.1.call-start = ((), (), s32[]{:S(2)}) async-start(), calls=%async_computation.83 | async-start | bytes 2621440 | tf_op jit(solution)/shard_map/reduce_scatter | solution.py:115
  1222.2 159.4 %all-gather.69.cloned.1.call-start = ((), (), s32[]{:S(2)}) async-start(), calls=%async_computation.92 | async-start | bytes 1310720 | tf_op jit(solution)/shard_map/all_gather | solution.py:111
  1367.3 143.5 %all-reduce.53.cloned.1.call-start = ((), (), s32[]{:S(2)}) async-start(), calls=%async_computation.131 | async-start | bytes 2097152 | tf_op jit(solution)/shard_map/psum | solution.py:287
  1442.8 157.6 %reduce-scatter.179.cloned.1.call-start = ((), (), s32[]{:S(2)}) async-start(), calls=%async_computation.129 | async-start | bytes 2359296
  1448.2 173.0 %reduce-scatter.177.cloned.1.call-start = ((), (), s32[]{:S(2)}) async-start(), calls=%async_computation.128 | async-start | bytes 2359296
  1454.6 236.8 %reduce-scatter.175.cloned.1.call-start = ((), (), s32[]{:S(2)}) async-start(), calls=%async_computation.127 | async-start | bytes 2359296
  1460.9 300.7 %reduce-scatter.173.cloned.1.call-start = ((), (), s32[]{:S(2)}) async-start(), calls=%async_computation.126 | async-start | bytes 2359296
  1467.2 364.4 %reduce-scatter.155.cloned.1.call-start = ((), (), s32[]{:S(2)}) async-start(), calls=%async_computation.113 | async-start | bytes 2359296 | tf_op jit(solution)/shard_map/reduce_scatter | solution.py:101
  1471.5 430.4 %reduce-scatter.153.cloned.1.call-start = ((), (), s32[]{:S(2)}) async-start(), calls=%async_computation.112 | async-start | bytes 2359296 | tf_op jit(solution)/shard_map/reduce_scatter | solution.py:101
  1475.7 496.5 %reduce-scatter.151.cloned.1.call-start = ((), (), s32[]{:S(2)}) async-start(), calls=%async_computation.111 | async-start | bytes 2359296 | tf_op jit(solution)/shard_map/reduce_scatter | solution.py:101
  1479.8 562.6 %reduce-scatter.149.cloned.1.call-start = ((), (), s32[]{:S(2)}) async-start(), calls=%async_computation.110 | async-start | bytes 2359296 | tf_op jit(solution)/shard_map/reduce_scatter | solution.py:101
  1484.0 623.3 %reduce-scatter.171.cloned.1.call-start = ((), (), s32[]{:S(2)}) async-start(), calls=%async_computation.125 | async-start | bytes 589824
  1486.8 685.0 %reduce-scatter.165.cloned.1.call-start = ((), (), s32[]{:S(2)}) async-start(), calls=%async_computation.122 | async-start | bytes 589824
  1488.3 747.6 %reduce-scatter.169.cloned.1.call-start = ((), (), s32[]{:S(2)}) async-start(), calls=%async_computation.124 | async-start | bytes 589824
  1489.9 810.7 %reduce-scatter.167.cloned.1.call-start = ((), (), s32[]{:S(2)}) async-start(), calls=%async_computation.123 | async-start | bytes 589824
  1491.5 877.1 %reduce-scatter.145.cloned.1.call-start = ((), (), s32[]{:S(2)}) async-start(), calls=%async_computation.108 | async-start | bytes 1769472 | tf_op jit(solution)/shard_map/reduce_scatter | solution.py:89
  1495.0 941.9 %reduce-scatter.143.cloned.1.call-start = ((), (), s32[]{:S(2)}) async-start(), calls=%async_computation.107 | async-start | bytes 1769472 | tf_op jit(solution)/shard_map/reduce_scatter | solution.py:89
  1498.6 1006.1 %reduce-scatter.141.cloned.1.call-start = ((), (), s32[]{:S(2)}) async-start(), calls=%async_computation.106 | async-start | bytes 1769472 | tf_op jit(solution)/shard_map/reduce_scatter | solution.py:89
  1502.3 1070.8 %reduce-scatter.147.cloned.1.call-start = ((), (), s32[]{:S(2)}) async-start(), calls=%async_computation.109 | async-start | bytes 1769472 | tf_op jit(solution)/shard_map/reduce_scatter | solution.py:89
  1504.6 1132.7 %reduce-scatter.127.cloned.1.call-start = ((), (), s32[]{:S(2)}) async-start(), calls=%async_computation.99 | async-start | bytes 589824 | tf_op jit(solution)/shard_map/reduce_scatter | solution.py:77
  1505.8 1196.0 %reduce-scatter.129.cloned.1.call-start = ((), (), s32[]{:S(2)}) async-start(), calls=%async_computation.100 | async-start | bytes 589824 | tf_op jit(solution)/shard_map/reduce_scatter | solution.py:77
  1507.0 1258.9 %reduce-scatter.125.cloned.1.call-start = ((), (), s32[]{:S(2)}) async-start(), calls=%async_computation.98 | async-start | bytes 589824 | tf_op jit(solution)/shard_map/reduce_scatter | solution.py:77
  1509.3 1321.4 %reduce-scatter.131.cloned.1.call-start = ((), (), s32[]{:S(2)}) async-start(), calls=%async_computation.101 | async-start | bytes 589824 | tf_op jit(solution)/shard_map/reduce_scatter | solution.py:77
  1510.7 1385.8 %reduce-scatter.117.cloned.1.call-start = ((), (), s32[]{:S(2)}) async-start(), calls=%async_computation.91 | async-start | bytes 1179648 | tf_op jit(solution)/shard_map/reduce_scatter | solution.py:71
  1523.7 1438.9 %reduce-scatter.119.cloned.1.call-start = ((), (), s32[]{:S(2)}) async-start(), calls=%async_computation.93 | async-start | bytes 1179648 | tf_op jit(solution)/shard_map/reduce_scatter | solution.py:71
  1537.6 1490.9 %reduce-scatter.121.cloned.1.call-start = ((), (), s32[]{:S(2)}) async-start(), calls=%async_computation.95 | async-start | bytes 1179648 | tf_op jit(solution)/shard_map/reduce_scatter | solution.py:71
  1550.6 1543.8 %reduce-scatter.123.cloned.1.call-start = ((), (), s32[]{:S(2)}) async-start(), calls=%async_computation.97 | async-start | bytes 1179648 | tf_op jit(solution)/shard_map/reduce_scatter | solution.py:71
  1564.9 1596.6 %reduce-scatter.157.cloned.1.call-start = ((), (), s32[]{:S(2)}) async-start(), calls=%async_computation.118 | async-start | bytes 1769472
  1571.3 1657.6 %reduce-scatter.159.cloned.1.call-start = ((), (), s32[]{:S(2)}) async-start(), calls=%async_computation.119 | async-start | bytes 1769472
  1577.7 1718.4 %reduce-scatter.161.cloned.1.call-start = ((), (), s32[]{:S(2)}) async-start(), calls=%async_computation.120 | async-start | bytes 1769472
  1584.1 1779.5 %reduce-scatter.163.cloned.1.call-start = ((), (), s32[]{:S(2)}) async-start(), calls=%async_computation.121 | async-start | bytes 1769472
  1590.6 1843.8 %reduce-scatter.135.cloned.1.call-start = ((), (), s32[]{:S(2)}) async-start(), calls=%async_computation.103 | async-start | bytes 2359296 | tf_op jit(solution)/shard_map/reduce_scatter | solution.py:80
  1593.0 1912.2 %reduce-scatter.137.cloned.1.call-start = ((), (), s32[]{:S(2)}) async-start(), calls=%async_computation.104 | async-start | bytes 2359296 | tf_op jit(solution)/shard_map/reduce_scatter | solution.py:80
  1595.2 1980.9 %reduce-scatter.133.cloned.1.call-start = ((), (), s32[]{:S(2)}) async-start(), calls=%async_computation.102 | async-start | bytes 2359296 | tf_op jit(solution)/shard_map/reduce_scatter | solution.py:80
  1597.4 2049.5 %reduce-scatter.139.cloned.1.call-start = ((), (), s32[]{:S(2)}) async-start(), calls=%async_computation.105 | async-start | bytes 2359296 | tf_op jit(solution)/shard_map/reduce_scatter | solution.py:80
  (250 other events, 20175.1 us)
Sparse Core Ops, SparseCore 0:
  10.1 42.8 all-gather.30
  55.1 44.4 all-gather.32
  110.5 51.0 all-reduce.50
  163.7 51.1 all-gather.34
  218.7 29.6 reduce-scatter.76
  250.7 31.4 reduce-scatter.82
  284.9 31.4 reduce-scatter.88
  318.9 31.4 reduce-scatter.94
  352.8 49.4 all-gather.38
  479.4 31.4 reduce-scatter.96
  513.3 31.4 reduce-scatter.90
  547.3 31.4 reduce-scatter.84
  581.1 31.4 reduce-scatter.78
  614.8 49.2 all-gather.42
  702.3 51.0 all-gather.44
  828.7 16.8 all-gather.40
  866.6 31.4 reduce-scatter.112
  900.6 31.4 reduce-scatter.108
  934.6 31.4 reduce-scatter.104
  968.6 31.4 reduce-scatter.100
  1002.8 31.4 reduce-scatter.98
  1036.6 31.4 reduce-scatter.80
  1070.8 31.4 reduce-scatter.92
  1104.8 31.4 reduce-scatter.86
  1138.3 16.8 all-gather.64
  1213.7 31.4 reduce-scatter.114
  1247.7 31.4 reduce-scatter.102
  1281.9 31.4 reduce-scatter.110
  1315.7 31.4 reduce-scatter.106
  1363.6 17.8 all-gather.68
  1420.3 16.8 all-gather.72
  1442.9 36.5 all-reduce.52
  1482.8 68.3 reduce-scatter.178
  1554.7 66.5 reduce-scatter.176
  1624.7 66.6 reduce-scatter.174
  1694.9 66.6 reduce-scatter.172
  1765.0 66.6 reduce-scatter.154
  1835.2 66.7 reduce-scatter.152
  1905.5 66.6 reduce-scatter.150
  1975.7 66.6 reduce-scatter.148
  2046.3 60.8 reduce-scatter.170
  2110.8 60.9 reduce-scatter.164
  2175.0 60.8 reduce-scatter.168
  2239.6 61.0 reduce-scatter.166
  2304.1 64.4 reduce-scatter.144
  2372.5 64.4 reduce-scatter.142
  2440.3 64.4 reduce-scatter.140
  2508.5 64.5 reduce-scatter.146
  2576.4 60.8 reduce-scatter.126
  2640.8 60.9 reduce-scatter.128
  2705.0 60.9 reduce-scatter.124
  2769.6 60.9 reduce-scatter.130
  2834.1 62.3 reduce-scatter.116
  2900.1 62.4 reduce-scatter.118
  2966.1 62.3 reduce-scatter.120
  3032.1 62.3 reduce-scatter.122
  3097.7 63.7 reduce-scatter.156
  3165.2 63.7 reduce-scatter.158
  3232.4 63.7 reduce-scatter.160
  3299.8 63.7 reduce-scatter.162
  3367.1 67.2 reduce-scatter.134
  3438.0 67.1 reduce-scatter.136
  3508.7 67.3 reduce-scatter.132
  3579.7 67.1 reduce-scatter.138
  (16 shorter events, 263.8 us)
where the time goes:
time: 3670 us; the launch traced here: 3660 us
  waiting for transfers between devices  2990 us (81%)
  matrix products  239 us (7%)
  local copies, waits for them, and re-layouts  152 us (4%)
  blocking collectives  141 us (4%)
  other arithmetic  64.4 us (2%)
  starting transfers between devices  47.6 us (1%)
    unnamed x92, waiting for transfers between devices  686 us
    reduce_scatter x20, waiting for transfers between devices, share_rows(): return lax.psum_scatter(value, 'cond', scatter_dimension=1, tiled=True)  554 us
    reduce_scatter x4, waiting for transfers between devices, spread_grads(): lax.psum_scatter(gradients[3].astype(jnp.bfloat16), 'seq', scatter_dimens...  281 us
    reduce_scatter x4, waiting for transfers between devices, spread_grads(): lax.psum_scatter(gradients[10].astype(jnp.bfloat16), 'seq', scatter_dimen...  278 us
    reduce_scatter x4, waiting for transfers between devices, spread_grads(): lax.psum_scatter(gradients[6].astype(jnp.bfloat16), 'seq', scatter_dimens...  271 us
    reduce_scatter x4, waiting for transfers between devices, spread_grads(): lax.psum_scatter(gradients[0].astype(jnp.bfloat16), 'seq', scatter_dimens...  262 us
    reduce_scatter x4, waiting for transfers between devices, spread_grads(): lax.psum_scatter(gradients[2].astype(jnp.bfloat16), 'seq', scatter_dimens...  232 us
    all_gather x20, waiting for transfers between devices, gather_rows(): return lax.all_gather(value, 'cond', axis=1, tiled=True)  185 us
  transfers between devices with their start and end apart: 96, of which 85 were waited for; matrix products, arithmetic and copies ran while one was open for 11% of the time, Pallas kernels for 0%

commit v1 on v0

--- a/solution.py
+++ b/solution.py
@@ -1,3 +1,4 @@
+import functools
 import math
 import jax
 import jax.numpy as jnp
@@ -9,6 +10,47 @@
 CONV_DILATION = 27
 EPSILON = 1e-05
 NEG_FILL = -1e30
+
+
+def quotas_watch(sheet, peer_axis):
+    all_rows = []
+    x_next, t_next, view_out = (
+        jax.lax.psum(1, peer_axis),
+        jax.lax.axis_index(peer_axis),
+        sheet.shape[1],
+    )
+    for k, k0 in enumerate(sheet.shape):
+        all_rows.append(k0 * x_next if k == 1 else k0)
+    local_now = a_now = sheet
+    s = 1
+    last = lax.dynamic_update_slice_in_dim(
+        jnp.zeros(all_rows, sheet.dtype), sheet, t_next * view_out, axis=1
+    )
+    while s < x_next // 2 + 1:
+        line_up = []
+        k = 0
+        while k < x_next:
+            line_up.append((k, (k + 1) % x_next))
+            k += 1
+        local_now = jax.lax.ppermute(local_now, peer_axis, line_up)
+        last = lax.dynamic_update_slice_in_dim(
+            last, local_now, (t_next - s) % x_next * view_out, axis=1
+        )
+        if 2 * s < x_next:
+            ledger = []
+            k = 0
+            while k < x_next:
+                ledger.append((k, (k - 1) % x_next))
+                k = k + 1
+            a_now = jax.lax.ppermute(a_now, peer_axis, ledger)
+            last = lax.dynamic_update_slice_in_dim(
+                last, a_now, (t_next + s) % x_next * view_out, axis=1
+            )
+        s = s + 1
+    return last
+
+
+proceed_plate_for = functools.partial(quotas_watch, peer_axis="cond")
 
 
 def extended(cells, sides, width):
@@ -108,7 +150,7 @@
 
 
 def gather_rows(value):
-    return lax.all_gather(value, "cond", axis=1, tiled=True)
+    return proceed_plate_for(value)
 
 
 def share_rows(value):

time: 3670 us -> 3460 us (0.943)
  waiting for transfers between devices: 2990 us -> 2680 us
  starting transfers between devices: 47.6 us -> 106 us
  local copies, waits for them, and re-layouts: 152 us -> 210 us
    reduce_scatter x20, waiting for transfers between devices: 554 us -> 297 us  [share_rows(): return lax.psum_scatter(value, 'cond', scatter_dimension=1, tiled=True)]
    all_gather x20 -> x0, waiting for transfers between devices: 185 us -> none  [gather_rows(): return lax.all_gather(value, 'cond', axis=1, tiled=True)]
    ppermute x0 -> x60, waiting for transfers between devices: none -> 165 us  [the longest x40 146 us: quotas_watch(): local_now = jax.lax.ppermute(local_now, peer_axis, line_up)]
    ppermute x0 -> x60, starting transfers between devices: none -> 59.6 us  [the longest x40 35.6 us: quotas_watch(): local_now = jax.lax.ppermute(local_now, peer_axis, line_up)]
    unnamed x485 -> x573, local copies, waits for them, and re-layouts: 76.7 us -> 89.5 us
    unnamed x92 -> x72, waiting for transfers between devices: 686 us -> 675 us
  transfers between devices with their start and end apart: 96 -> 136, of which waited for: 85 -> 91; matrix products, arithmetic and copies ran while one was open for 11% -> 11% of each run, Pallas kernels for 0% -> 0%
where the time goes in v1:
time: 3460 us; the launch traced here: 3450 us
  waiting for transfers between devices  2680 us (77%)
  matrix products  217 us (6%)
  local copies, waits for them, and re-layouts  210 us (6%)
  blocking collectives  143 us (4%)
  starting transfers between devices  106 us (3%)
  other arithmetic  69.5 us (2%)
    unnamed x72, waiting for transfers between devices  675 us
    reduce_scatter x20, waiting for transfers between devices, share_rows(): return lax.psum_scatter(value, 'cond', scatter_dimension=1, tiled=True)  297 us
    reduce_scatter x4, waiting for transfers between devices, spread_grads(): lax.psum_scatter(gradients[3].astype(jnp.bfloat16), 'seq', scatter_dimens...  281 us
    reduce_scatter x4, waiting for transfers between devices, spread_grads(): lax.psum_scatter(gradients[10].astype(jnp.bfloat16), 'seq', scatter_dimen...  277 us
    reduce_scatter x4, waiting for transfers between devices, spread_grads(): lax.psum_scatter(gradients[6].astype(jnp.bfloat16), 'seq', scatter_dimens...  271 us
    reduce_scatter x4, waiting for transfers between devices, spread_grads(): lax.psum_scatter(gradients[0].astype(jnp.bfloat16), 'seq', scatter_dimens...  262 us
    reduce_scatter x4, waiting for transfers between devices, spread_grads(): lax.psum_scatter(gradients[2].astype(jnp.bfloat16), 'seq', scatter_dimens...  232 us
    ppermute x40, waiting for transfers between devices, quotas_watch(): local_now = jax.lax.ppermute(local_now, peer_axis, line_up)  146 us
  transfers between devices with their start and end apart: 136, of which 91 were waited for; matrix products, arithmetic and copies ran while one was open for 11% of the time, Pallas kernels for 0%

profile of v1, /device:TPU:0, one launch (start us, length us, event | category | flops | bytes accessed | tf_op | source)
XLA Modules:
  0.0 3448.0 jit_solution(5862453600844652258)
XLA Ops:
  9.6 43.5 %all-gather.7.cloned.1.call-done = bf16[2048,256]{1,0:T(8,128)(2,1)} async-done(((bf16[256,256]{1,0:T(8,128)(2,1)}), bf16[2048,256]{1,0:T(8,128)(2,1)}) %all-gather.7.cloned.1.call-update) | async-done | bytes 1048592 | tf_op jit(solution)/shard_map/all_gather | solution.py:96
  78.9 20.4 all-gather.9.cloned.1.call-done
  109.5 31.4 all_gather.26
  140.9 19.0 all-reduce.51.cloned.1.call-done
  164.6 48.5 %all-gather.11.cloned.1.call-done = bf16[256,4096]{1,0:T(8,128)(2,1)} async-done(((bf16[256,512]{1,0:T(8,128)(2,1)}), bf16[256,4096]{1,0:T(8,128)(2,1)}) %all-gather.11.cloned.1.call-update) | async-done | bytes 2097168 | tf_op jit(solution)/shard_map/all_gather | solution.py:99
  244.2 19.8 all-reduce.46
  264.1 16.4 reduce-scatter.95.cloned.1.call-done
  280.5 34.2 reduce-scatter.83.cloned.1.call-done
  314.7 34.0 reduce-scatter.77.cloned.1.call-done
  351.1 10.7 all-reduce.43
  370.0 31.1 all_gather.31
  479.2 9.3 collective-permute-done.26
  514.2 12.0 collective-permute-done.38
  531.7 32.5 reduce-scatter.97.cloned.1.call-done
  565.5 10.1 all-reduce.42
  592.7 23.1 all-gather.15.cloned.1.call-done
  620.3 47.2 %all-gather.17.cloned.1.call-done = bf16[1024,1024]{1,0:T(8,128)(2,1)} async-done(((bf16[1024,128]{1,0:T(8,128)(2,1)}), bf16[1024,1024]{1,0:T(8,128)(2,1)}) %all-gather.17.cloned.1.call-update) | async-done | bytes 2097168 | tf_op jit(solution)/shard_map/all_gather | solution.py:107
  667.5 8.8 add_convert_fusion.2
  693.6 10.4 collective-permute-done.21
  704.2 11.2 collective-permute-done.23
  718.1 6.8 add_convert_fusion.1
  738.1 10.2 collective-permute-done.51
  748.3 9.7 collective-permute-done.29
  766.8 6.8 add_convert_fusion
  795.6 9.2 collective-permute-done.5
  835.4 34.0 reduce-scatter.99.cloned.1.call-done
  869.4 34.0 reduce-scatter.113.cloned.1.call-done
  903.4 34.2 reduce-scatter.81.cloned.1.call-done
  937.5 34.0 reduce-scatter.101.cloned.1.call-done
  975.4 10.3 all-reduce.41
  1135.1 33.9 reduce-scatter.103.cloned.1.call-done
  1172.3 10.1 all-reduce.40
  1399.2 14.6 reduce-scatter.177.cloned.1.call-done
  1414.9 69.3 %reduce-scatter.179.cloned.1.call-done = bf16[128,1024]{1,0:T(8,128)(2,1)} async-done(((bf16[1024,1024]{1,0:T(8,128)(2,1)}), bf16[128,1024]{1,0:T(8,128)(2,1)}) %reduce-scatter.179.cloned.1.call-update) | async-done | bytes 262160
  1485.4 69.5 %reduce-scatter.173.cloned.1.call-done = bf16[128,1024]{1,0:T(8,128)(2,1)} async-done(((bf16[1024,1024]{1,0:T(8,128)(2,1)}), bf16[128,1024]{1,0:T(8,128)(2,1)}) %reduce-scatter.173.cloned.1.call-update) | async-done | bytes 262160
  1558.2 66.8 %reduce-scatter.151.cloned.1.call-done = bf16[128,1024]{1,0:T(8,128)(2,1)} async-done(((bf16[1024,1024]{1,0:T(8,128)(2,1)}), bf16[128,1024]{1,0:T(8,128)(2,1)}) %reduce-scatter.151.cloned.1.call-update) | async-done | bytes 262160 | tf_op jit(solution)/shard_map/reduce_scatter | solution.py:143
  1625.0 70.1 %reduce-scatter.153.cloned.1.call-done = bf16[128,1024]{1,0:T(8,128)(2,1)} async-done(((bf16[1024,1024]{1,0:T(8,128)(2,1)}), bf16[128,1024]{1,0:T(8,128)(2,1)}) %reduce-scatter.153.cloned.1.call-update) | async-done | bytes 262160 | tf_op jit(solution)/shard_map/reduce_scatter | solution.py:143
  1695.2 70.3 %reduce-scatter.155.cloned.1.call-done = bf16[128,1024]{1,0:T(8,128)(2,1)} async-done(((bf16[1024,1024]{1,0:T(8,128)(2,1)}), bf16[128,1024]{1,0:T(8,128)(2,1)}) %reduce-scatter.155.cloned.1.call-update) | async-done | bytes 262160 | tf_op jit(solution)/shard_map/reduce_scatter | solution.py:143
  1765.5 70.0 %reduce-scatter.149.cloned.1.call-done = bf16[128,1024]{1,0:T(8,128)(2,1)} async-done(((bf16[1024,1024]{1,0:T(8,128)(2,1)}), bf16[128,1024]{1,0:T(8,128)(2,1)}) %reduce-scatter.149.cloned.1.call-update) | async-done | bytes 262160 | tf_op jit(solution)/shard_map/reduce_scatter | solution.py:143
  1837.6 62.0 %reduce-scatter.167.cloned.1.call-done = bf16[128,256]{1,0:T(8,128)(2,1)} async-done(((bf16[1024,256]{1,0:T(8,128)(2,1)}), bf16[128,256]{1,0:T(8,128)(2,1)}) %reduce-scatter.167.cloned.1.call-update) | async-done | bytes 65552
  1900.6 63.7 %reduce-scatter.169.cloned.1.call-done = bf16[128,256]{1,0:T(8,128)(2,1)} async-done(((bf16[1024,256]{1,0:T(8,128)(2,1)}), bf16[128,256]{1,0:T(8,128)(2,1)}) %reduce-scatter.169.cloned.1.call-update) | async-done | bytes 65552
  1965.3 63.1 %reduce-scatter.165.cloned.1.call-done = bf16[128,256]{1,0:T(8,128)(2,1)} async-done(((bf16[1024,256]{1,0:T(8,128)(2,1)}), bf16[128,256]{1,0:T(8,128)(2,1)}) %reduce-scatter.165.cloned.1.call-update) | async-done | bytes 65552
  2029.3 63.9 %reduce-scatter.171.cloned.1.call-done = bf16[128,256]{1,0:T(8,128)(2,1)} async-done(((bf16[1024,256]{1,0:T(8,128)(2,1)}), bf16[128,256]{1,0:T(8,128)(2,1)}) %reduce-scatter.171.cloned.1.call-update) | async-done | bytes 65552
  2094.8 66.4 %reduce-scatter.143.cloned.1.call-done = bf16[128,3,256]{2,0,1:T(8,128)(2,1)} async-done(((bf16[1024,3,256]{2,0,1:T(8,128)(2,1)}), bf16[128,3,256]{2,0,1:T(8,128)(2,1)}) %reduce-scatter.143.cloned.1.call-update) | async-done | bytes 196624 | tf_op jit(solution)/shard_map/reduce_scatter | solution.py:131
  2161.2 68.3 %reduce-scatter.145.cloned.1.call-done = bf16[128,3,256]{2,0,1:T(8,128)(2,1)} async-done(((bf16[1024,3,256]{2,0,1:T(8,128)(2,1)}), bf16[128,3,256]{2,0,1:T(8,128)(2,1)}) %reduce-scatter.145.cloned.1.call-update) | async-done | bytes 196624 | tf_op jit(solution)/shard_map/reduce_scatter | solution.py:131
  2229.5 67.8 %reduce-scatter.141.cloned.1.call-done = bf16[128,3,256]{2,0,1:T(8,128)(2,1)} async-done(((bf16[1024,3,256]{2,0,1:T(8,128)(2,1)}), bf16[128,3,256]{2,0,1:T(8,128)(2,1)}) %reduce-scatter.141.cloned.1.call-update) | async-done | bytes 196624 | tf_op jit(solution)/shard_map/reduce_scatter | solution.py:131
  2297.3 68.2 %reduce-scatter.147.cloned.1.call-done = bf16[128,3,256]{2,0,1:T(8,128)(2,1)} async-done(((bf16[1024,3,256]{2,0,1:T(8,128)(2,1)}), bf16[128,3,256]{2,0,1:T(8,128)(2,1)}) %reduce-scatter.147.cloned.1.call-update) | async-done | bytes 196624 | tf_op jit(solution)/shard_map/reduce_scatter | solution.py:131
  2367.6 19.8 all-reduce.45
  2390.9 38.6 %reduce-scatter.125.cloned.1.call-done = bf16[128,256]{1,0:T(8,128)(2,1)} async-done(((bf16[1024,256]{1,0:T(8,128)(2,1)}), bf16[128,256]{1,0:T(8,128)(2,1)}) %reduce-scatter.125.cloned.1.call-update) | async-done | bytes 65552 | tf_op jit(solution)/shard_map/reduce_scatter | solution.py:119
  2429.6 64.4 %reduce-scatter.127.cloned.1.call-done = bf16[128,256]{1,0:T(8,128)(2,1)} async-done(((bf16[1024,256]{1,0:T(8,128)(2,1)}), bf16[128,256]{1,0:T(8,128)(2,1)}) %reduce-scatter.127.cloned.1.call-update) | async-done | bytes 65552 | tf_op jit(solution)/shard_map/reduce_scatter | solution.py:119
  2494.0 64.2 %reduce-scatter.129.cloned.1.call-done = bf16[128,256]{1,0:T(8,128)(2,1)} async-done(((bf16[1024,256]{1,0:T(8,128)(2,1)}), bf16[128,256]{1,0:T(8,128)(2,1)}) %reduce-scatter.129.cloned.1.call-update) | async-done | bytes 65552 | tf_op jit(solution)/shard_map/reduce_scatter | solution.py:119
  2558.2 64.6 %reduce-scatter.131.cloned.1.call-done = bf16[128,256]{1,0:T(8,128)(2,1)} async-done(((bf16[1024,256]{1,0:T(8,128)(2,1)}), bf16[128,256]{1,0:T(8,128)(2,1)}) %reduce-scatter.131.cloned.1.call-update) | async-done | bytes 65552 | tf_op jit(solution)/shard_map/reduce_scatter | solution.py:119
  2624.4 64.0 %reduce-scatter.117.cloned.1.call-done = bf16[256,256]{1,0:T(8,128)(2,1)} async-done(((bf16[2048,256]{1,0:T(8,128)(2,1)}), bf16[256,256]{1,0:T(8,128)(2,1)}) %reduce-scatter.117.cloned.1.call-update) | async-done | bytes 131088 | tf_op jit(solution)/shard_map/reduce_scatter | solution.py:113
  2688.3 66.3 %reduce-scatter.119.cloned.1.call-done = bf16[256,256]{1,0:T(8,128)(2,1)} async-done(((bf16[2048,256]{1,0:T(8,128)(2,1)}), bf16[256,256]{1,0:T(8,128)(2,1)}) %reduce-scatter.119.cloned.1.call-update) | async-done | bytes 131088 | tf_op jit(solution)/shard_map/reduce_scatter | solution.py:113
  2754.6 65.8 %reduce-scatter.121.cloned.1.call-done = bf16[256,256]{1,0:T(8,128)(2,1)} async-done(((bf16[2048,256]{1,0:T(8,128)(2,1)}), bf16[256,256]{1,0:T(8,128)(2,1)}) %reduce-scatter.121.cloned.1.call-update) | async-done | bytes 131088 | tf_op jit(solution)/shard_map/reduce_scatter | solution.py:113
  2820.4 66.3 %reduce-scatter.123.cloned.1.call-done = bf16[256,256]{1,0:T(8,128)(2,1)} async-done(((bf16[2048,256]{1,0:T(8,128)(2,1)}), bf16[256,256]{1,0:T(8,128)(2,1)}) %reduce-scatter.123.cloned.1.call-update) | async-done | bytes 131088 | tf_op jit(solution)/shard_map/reduce_scatter | solution.py:113
  2888.5 65.3 %reduce-scatter.157.cloned.1.call-done = bf16[128,768]{1,0:T(8,128)(2,1)} async-done(((bf16[1024,768]{1,0:T(8,128)(2,1)}), bf16[128,768]{1,0:T(8,128)(2,1)}) %reduce-scatter.157.cloned.1.call-update) | async-done | bytes 196624
  2955.0 66.3 %reduce-scatter.159.cloned.1.call-done = bf16[128,768]{1,0:T(8,128)(2,1)} async-done(((bf16[1024,768]{1,0:T(8,128)(2,1)}), bf16[128,768]{1,0:T(8,128)(2,1)}) %reduce-scatter.159.cloned.1.call-update) | async-done | bytes 196624
  3022.5 66.0 %reduce-scatter.161.cloned.1.call-done = bf16[128,768]{1,0:T(8,128)(2,1)} async-done(((bf16[1024,768]{1,0:T(8,128)(2,1)}), bf16[128,768]{1,0:T(8,128)(2,1)}) %reduce-scatter.161.cloned.1.call-update) | async-done | bytes 196624
  3089.7 66.4 %reduce-scatter.163.cloned.1.call-done = bf16[128,768]{1,0:T(8,128)(2,1)} async-done(((bf16[1024,768]{1,0:T(8,128)(2,1)}), bf16[128,768]{1,0:T(8,128)(2,1)}) %reduce-scatter.163.cloned.1.call-update) | async-done | bytes 196624
  3158.2 68.7 %reduce-scatter.133.cloned.1.call-done = bf16[256,512]{1,0:T(8,128)(2,1)} async-done(((bf16[256,4096]{1,0:T(8,128)(2,1)}), bf16[256,512]{1,0:T(8,128)(2,1)}) %reduce-scatter.133.cloned.1.call-update) | async-done | bytes 262160 | tf_op jit(solution)/shard_map/reduce_scatter | solution.py:122
  3226.9 70.5 %reduce-scatter.135.cloned.1.call-done = bf16[256,512]{1,0:T(8,128)(2,1)} async-done(((bf16[256,4096]{1,0:T(8,128)(2,1)}), bf16[256,512]{1,0:T(8,128)(2,1)}) %reduce-scatter.135.cloned.1.call-update) | async-done | bytes 262160 | tf_op jit(solution)/shard_map/reduce_scatter | solution.py:122
  3297.3 70.7 %reduce-scatter.137.cloned.1.call-done = bf16[256,512]{1,0:T(8,128)(2,1)} async-done(((bf16[256,4096]{1,0:T(8,128)(2,1)}), bf16[256,512]{1,0:T(8,128)(2,1)}) %reduce-scatter.137.cloned.1.call-update) | async-done | bytes 262160 | tf_op jit(solution)/shard_map/reduce_scatter | solution.py:122
  3368.0 70.8 %reduce-scatter.139.cloned.1.call-done = bf16[256,512]{1,0:T(8,128)(2,1)} async-done(((bf16[256,4096]{1,0:T(8,128)(2,1)}), bf16[256,512]{1,0:T(8,128)(2,1)}) %reduce-scatter.139.cloned.1.call-update) | async-done | bytes 262160 | tf_op jit(solution)/shard_map/reduce_scatter | solution.py:122
  (1234 shorter events, 707.8 us)
Async XLA Ops:
  7.2 45.8 %all-gather.7.cloned.1.call-start = ((), (), s32[]{:S(2)}) async-start(), calls=%async_computation.52 | async-start | bytes 1179648 | tf_op jit(solution)/shard_map/all_gather | solution.py:96
  7.9 91.4 %all-gather.9.cloned.1.call-start = ((), (), s32[]{:S(2)}) async-start(), calls=%async_computation.53 | async-start | bytes 1769472 | tf_op jit(solution)/shard_map/all_gather | solution.py:97
  8.7 151.2 %all-reduce.51.cloned.1.call-start = ((), (), s32[]{:S(2)}) async-start(), calls=%async_computation.110 | async-start | bytes 4194304 | tf_op jit(solution)/shard_map/psum | solution.py:223
  60.0 42.0 %collective-permute-start.8 = (bf16[27,256]{1,0:T(8,128)(2,1)S(1)}, bf16[27,256]{1,0:T(8,128)(2,1)S(1)}, u32[]{:S(2)}, u32[]{:S(2)}) collective-permute-start(bf16[27,256]{1,0:T(8,128)(2,1)S(1)} %get-tuple-element.253), channel_id=1, source_target_pairs={{0,1},{1,2},{2,3},{3,4},{4,5},{5,6},{6,7},{8,9},{9,10},{10,11},{11... | collective-permute-start | bytes 41480 | tf_op jit(solution)/shard_map/ppermute | solution.py:64
  64.6 38.7 %collective-permute-start.9 = (bf16[27,256]{1,0:T(8,128)(2,1)S(1)}, bf16[27,256]{1,0:T(8,128)(2,1)S(1)}, u32[]{:S(2)}, u32[]{:S(2)}) collective-permute-start(bf16[27,256]{1,0:T(8,128)(2,1)S(1)} %get-tuple-element.254), channel_id=1, source_target_pairs={{1,0},{2,1},{3,2},{4,3},{5,4},{6,5},{7,6},{9,8},{10,9},{11,10},{12... | collective-permute-start | bytes 41480 | tf_op jit(solution)/shard_map/ppermute | solution.py:66
  108.9 104.3 %all-gather.11.cloned.1.call-start = ((), (), s32[]{:S(2)}) async-start(), calls=%async_computation.54 | async-start | bytes 2359296 | tf_op jit(solution)/shard_map/all_gather | solution.py:99
  109.4 154.6 %reduce-scatter.89.cloned.1.call-start = ((), (), s32[]{:S(2)}) async-start(), calls=%async_computation.64 | async-start | bytes 2621440 | tf_op jit(solution)/shard_map/reduce_scatter | solution.py:157
  216.9 63.6 %reduce-scatter.95.cloned.1.call-start = ((), (), s32[]{:S(2)}) async-start(), calls=%async_computation.67 | async-start | bytes 2621440 | tf_op jit(solution)/shard_map/reduce_scatter | solution.py:157
  223.2 91.4 %reduce-scatter.83.cloned.1.call-start = ((), (), s32[]{:S(2)}) async-start(), calls=%async_computation.61 | async-start | bytes 2621440 | tf_op jit(solution)/shard_map/reduce_scatter | solution.py:157
  234.7 113.9 %reduce-scatter.77.cloned.1.call-start = ((), (), s32[]{:S(2)}) async-start(), calls=%async_computation.55 | async-start | bytes 2621440 | tf_op jit(solution)/shard_map/reduce_scatter | solution.py:157
  241.2 162.1 %all-gather.13.cloned.1.call-start = ((), (), s32[]{:S(2)}) async-start(), calls=%async_computation.56 | async-start | bytes 1769472 | tf_op jit(solution)/shard_map/all_gather | solution.py:102
  241.9 284.3 %reduce-scatter.79.cloned.1.call-start = ((), (), s32[]{:S(2)}) async-start(), calls=%async_computation.57 | async-start | bytes 2621440 | tf_op jit(solution)/shard_map/reduce_scatter | solution.py:157
  420.1 107.4 %reduce-scatter.85.cloned.1.call-start = ((), (), s32[]{:S(2)}) async-start(), calls=%async_computation.62 | async-start | bytes 2621440 | tf_op jit(solution)/shard_map/reduce_scatter | solution.py:157
  447.5 82.3 %reduce-scatter.91.cloned.1.call-start = ((), (), s32[]{:S(2)}) async-start(), calls=%async_computation.65 | async-start | bytes 2621440 | tf_op jit(solution)/shard_map/reduce_scatter | solution.py:157
  477.0 87.3 %reduce-scatter.97.cloned.1.call-start = ((), (), s32[]{:S(2)}) async-start(), calls=%async_computation.68 | async-start | bytes 2621440 | tf_op jit(solution)/shard_map/reduce_scatter | solution.py:157
  509.1 106.7 %all-gather.15.cloned.1.call-start = ((), (), s32[]{:S(2)}) async-start(), calls=%async_computation.58 | async-start | bytes 2359296 | tf_op jit(solution)/shard_map/all_gather | solution.py:106
  509.6 157.8 %all-gather.17.cloned.1.call-start = ((), (), s32[]{:S(2)}) async-start(), calls=%async_computation.59 | async-start | bytes 2359296 | tf_op jit(solution)/shard_map/all_gather | solution.py:107
  510.2 318.7 %reduce-scatter.87.cloned.1.call-start = ((), (), s32[]{:S(2)}) async-start(), calls=%async_computation.63 | async-start | bytes 2621440 | tf_op jit(solution)/shard_map/reduce_scatter | solution.py:157
  512.4 70.7 %collective-permute-start.39 = (bf16[512,256]{1,0:T(8,128)(2,1)}, bf16[512,256]{1,0:T(8,128)(2,1)}, u32[]{:S(2)}, u32[]{:S(2)}) collective-permute-start(bf16[512,256]{1,0:T(8,128)(2,1)} %get-tuple-element.195), channel_id=1, source_target_pairs={{0,24},{8,0},{16,8},{24,16},{1,25},{9,1},{17,9},{25,17},{2,26},{10... | collective-permute-start | bytes 786440 | tf_op jit(solution)/shard_map/ppermute | solution.py:45
  526.2 59.1 %collective-permute-start.40 = (bf16[512,256]{1,0:T(8,128)(2,1)S(1)}, bf16[512,256]{1,0:T(8,128)(2,1)}, u32[]{:S(2)}, u32[]{:S(2)}) collective-permute-start(bf16[512,256]{1,0:T(8,128)(2,1)S(1)} %collective-permute-done.38), channel_id=1, source_target_pairs={{0,8},{8,16},{16,24},{24,0},{1,9},{9,17},{17,25},{25,1},{2,10},{10... | collective-permute-start | bytes 786440 | tf_op jit(solution)/shard_map/ppermute | solution.py:35
  680.7 148.3 %reduce-scatter.105.cloned.1.call-start = ((), (), s32[]{:S(2)}) async-start(), calls=%async_computation.72 | async-start | bytes 2621440 | tf_op jit(solution)/shard_map/reduce_scatter | solution.py:157
  685.4 145.9 %reduce-scatter.93.cloned.1.call-start = ((), (), s32[]{:S(2)}) async-start(), calls=%async_computation.66 | async-start | bytes 2621440 | tf_op jit(solution)/shard_map/reduce_scatter | solution.py:157
  729.0 106.3 %reduce-scatter.109.cloned.1.call-start = ((), (), s32[]{:S(2)}) async-start(), calls=%async_computation.74 | async-start | bytes 2621440 | tf_op jit(solution)/shard_map/reduce_scatter | solution.py:157
  733.9 135.5 %reduce-scatter.99.cloned.1.call-start = ((), (), s32[]{:S(2)}) async-start(), calls=%async_computation.69 | async-start | bytes 2621440 | tf_op jit(solution)/shard_map/reduce_scatter | solution.py:157
  777.7 125.7 %reduce-scatter.113.cloned.1.call-start = ((), (), s32[]{:S(2)}) async-start(), calls=%async_computation.76 | async-start | bytes 2621440 | tf_op jit(solution)/shard_map/reduce_scatter | solution.py:157
  782.4 155.2 %reduce-scatter.81.cloned.1.call-start = ((), (), s32[]{:S(2)}) async-start(), calls=%async_computation.60 | async-start | bytes 2621440 | tf_op jit(solution)/shard_map/reduce_scatter | solution.py:157
  824.3 147.3 %reduce-scatter.101.cloned.1.call-start = ((), (), s32[]{:S(2)}) async-start(), calls=%async_computation.70 | async-start | bytes 2621440 | tf_op jit(solution)/shard_map/reduce_scatter | solution.py:157
  828.9 300.9 %reduce-scatter.107.cloned.1.call-start = ((), (), s32[]{:S(2)}) async-start(), calls=%async_computation.73 | async-start | bytes 2621440 | tf_op jit(solution)/shard_map/reduce_scatter | solution.py:157
  1023.4 106.4 %reduce-scatter.111.cloned.1.call-start = ((), (), s32[]{:S(2)}) async-start(), calls=%async_computation.75 | async-start | bytes 2621440 | tf_op jit(solution)/shard_map/reduce_scatter | solution.py:157
  1060.7 74.3 %reduce-scatter.115.cloned.1.call-start = ((), (), s32[]{:S(2)}) async-start(), calls=%async_computation.77 | async-start | bytes 2621440 | tf_op jit(solution)/shard_map/reduce_scatter | solution.py:157
  1100.0 69.0 %reduce-scatter.103.cloned.1.call-start = ((), (), s32[]{:S(2)}) async-start(), calls=%async_computation.71 | async-start | bytes 2621440 | tf_op jit(solution)/shard_map/reduce_scatter | solution.py:157
  1129.7 178.0 %all-reduce.53.cloned.1.call-start = ((), (), s32[]{:S(2)}) async-start(), calls=%async_computation.111 | async-start | bytes 2097152 | tf_op jit(solution)/shard_map/psum | solution.py:329
  1234.4 163.7 %reduce-scatter.175.cloned.1.call-start = ((), (), s32[]{:S(2)}) async-start(), calls=%async_computation.107 | async-start | bytes 2359296
  1239.9 173.9 %reduce-scatter.177.cloned.1.call-start = ((), (), s32[]{:S(2)}) async-start(), calls=%async_computation.108 | async-start | bytes 2359296
  1245.5 238.7 %reduce-scatter.179.cloned.1.call-start = ((), (), s32[]{:S(2)}) async-start(), calls=%async_computation.109 | async-start | bytes 2359296
  1251.2 303.7 %reduce-scatter.173.cloned.1.call-start = ((), (), s32[]{:S(2)}) async-start(), calls=%async_computation.106 | async-start | bytes 2359296
  1256.7 368.3 %reduce-scatter.151.cloned.1.call-start = ((), (), s32[]{:S(2)}) async-start(), calls=%async_computation.95 | async-start | bytes 2359296 | tf_op jit(solution)/shard_map/reduce_scatter | solution.py:143
  1261.8 433.4 %reduce-scatter.153.cloned.1.call-start = ((), (), s32[]{:S(2)}) async-start(), calls=%async_computation.96 | async-start | bytes 2359296 | tf_op jit(solution)/shard_map/reduce_scatter | solution.py:143
  1266.0 499.5 %reduce-scatter.155.cloned.1.call-start = ((), (), s32[]{:S(2)}) async-start(), calls=%async_computation.97 | async-start | bytes 2359296 | tf_op jit(solution)/shard_map/reduce_scatter | solution.py:143
  1270.1 565.4 %reduce-scatter.149.cloned.1.call-start = ((), (), s32[]{:S(2)}) async-start(), calls=%async_computation.94 | async-start | bytes 2359296 | tf_op jit(solution)/shard_map/reduce_scatter | solution.py:143
  1274.3 625.3 %reduce-scatter.167.cloned.1.call-start = ((), (), s32[]{:S(2)}) async-start(), calls=%async_computation.103 | async-start | bytes 589824
  1278.8 685.5 %reduce-scatter.169.cloned.1.call-start = ((), (), s32[]{:S(2)}) async-start(), calls=%async_computation.104 | async-start | bytes 589824
  1283.2 745.1 %reduce-scatter.165.cloned.1.call-start = ((), (), s32[]{:S(2)}) async-start(), calls=%async_computation.102 | async-start | bytes 589824
  1286.6 806.6 %reduce-scatter.171.cloned.1.call-start = ((), (), s32[]{:S(2)}) async-start(), calls=%async_computation.105 | async-start | bytes 589824
  1289.1 872.1 %reduce-scatter.143.cloned.1.call-start = ((), (), s32[]{:S(2)}) async-start(), calls=%async_computation.91 | async-start | bytes 1769472 | tf_op jit(solution)/shard_map/reduce_scatter | solution.py:131
  1293.1 936.4 %reduce-scatter.145.cloned.1.call-start = ((), (), s32[]{:S(2)}) async-start(), calls=%async_computation.92 | async-start | bytes 1769472 | tf_op jit(solution)/shard_map/reduce_scatter | solution.py:131
  1295.3 1001.9 %reduce-scatter.141.cloned.1.call-start = ((), (), s32[]{:S(2)}) async-start(), calls=%async_computation.90 | async-start | bytes 1769472 | tf_op jit(solution)/shard_map/reduce_scatter | solution.py:131
  1299.2 1066.3 %reduce-scatter.147.cloned.1.call-start = ((), (), s32[]{:S(2)}) async-start(), calls=%async_computation.93 | async-start | bytes 1769472 | tf_op jit(solution)/shard_map/reduce_scatter | solution.py:131
  1302.6 1126.9 %reduce-scatter.125.cloned.1.call-start = ((), (), s32[]{:S(2)}) async-start(), calls=%async_computation.82 | async-start | bytes 589824 | tf_op jit(solution)/shard_map/reduce_scatter | solution.py:119
  1303.9 1190.1 %reduce-scatter.127.cloned.1.call-start = ((), (), s32[]{:S(2)}) async-start(), calls=%async_computation.83 | async-start | bytes 589824 | tf_op jit(solution)/shard_map/reduce_scatter | solution.py:119
  1305.1 1253.1 %reduce-scatter.129.cloned.1.call-start = ((), (), s32[]{:S(2)}) async-start(), calls=%async_computation.84 | async-start | bytes 589824 | tf_op jit(solution)/shard_map/reduce_scatter | solution.py:119
  1306.3 1316.4 %reduce-scatter.131.cloned.1.call-start = ((), (), s32[]{:S(2)}) async-start(), calls=%async_computation.85 | async-start | bytes 589824 | tf_op jit(solution)/shard_map/reduce_scatter | solution.py:119
  1307.7 1380.7 %reduce-scatter.117.cloned.1.call-start = ((), (), s32[]{:S(2)}) async-start(), calls=%async_computation.78 | async-start | bytes 1179648 | tf_op jit(solution)/shard_map/reduce_scatter | solution.py:113
  1320.9 1433.7 %reduce-scatter.119.cloned.1.call-start = ((), (), s32[]{:S(2)}) async-start(), calls=%async_computation.79 | async-start | bytes 1179648 | tf_op jit(solution)/shard_map/reduce_scatter | solution.py:113
  1335.4 1485.0 %reduce-scatter.121.cloned.1.call-start = ((), (), s32[]{:S(2)}) async-start(), calls=%async_computation.80 | async-start | bytes 1179648 | tf_op jit(solution)/shard_map/reduce_scatter | solution.py:113
  1348.9 1537.7 %reduce-scatter.123.cloned.1.call-start = ((), (), s32[]{:S(2)}) async-start(), calls=%async_computation.81 | async-start | bytes 1179648 | tf_op jit(solution)/shard_map/reduce_scatter | solution.py:113
  1362.8 1591.0 %reduce-scatter.157.cloned.1.call-start = ((), (), s32[]{:S(2)}) async-start(), calls=%async_computation.98 | async-start | bytes 1769472
  1369.1 1652.2 %reduce-scatter.159.cloned.1.call-start = ((), (), s32[]{:S(2)}) async-start(), calls=%async_computation.99 | async-start | bytes 1769472
  1375.5 1713.0 %reduce-scatter.161.cloned.1.call-start = ((), (), s32[]{:S(2)}) async-start(), calls=%async_computation.100 | async-start | bytes 1769472
  1381.9 1774.2 %reduce-scatter.163.cloned.1.call-start = ((), (), s32[]{:S(2)}) async-start(), calls=%async_computation.101 | async-start | bytes 1769472
  1388.4 1838.4 %reduce-scatter.133.cloned.1.call-start = ((), (), s32[]{:S(2)}) async-start(), calls=%async_computation.86 | async-start | bytes 2359296 | tf_op jit(solution)/shard_map/reduce_scatter | solution.py:122
  1390.8 1906.5 %reduce-scatter.135.cloned.1.call-start = ((), (), s32[]{:S(2)}) async-start(), calls=%async_computation.87 | async-start | bytes 2359296 | tf_op jit(solution)/shard_map/reduce_scatter | solution.py:122
  1393.0 1975.0 %reduce-scatter.137.cloned.1.call-start = ((), (), s32[]{:S(2)}) async-start(), calls=%async_computation.88 | async-start | bytes 2359296 | tf_op jit(solution)/shard_map/reduce_scatter | solution.py:122
  1395.2 2043.7 %reduce-scatter.139.cloned.1.call-start = ((), (), s32[]{:S(2)}) async-start(), calls=%async_computation.89 | async-start | bytes 2359296 | tf_op jit(solution)/shard_map/reduce_scatter | solution.py:122
  (334 other events, 18399.4 us)
Sparse Core Ops, SparseCore 0:
  10.1 42.8 all-gather.6
  55.1 44.1 all-gather.8
  109.0 50.8 all-reduce.50
  162.0 51.1 all-gather.10
  217.0 29.6 reduce-scatter.88
  249.0 31.4 reduce-scatter.94
  283.2 31.4 reduce-scatter.82
  317.2 31.4 reduce-scatter.76
  351.1 48.7 all-gather.12
  420.2 30.7 reduce-scatter.78
  453.5 34.4 reduce-scatter.84
  490.6 39.2 reduce-scatter.90
  532.4 31.8 reduce-scatter.96
  566.5 49.2 all-gather.14
  617.9 49.5 all-gather.16
  680.8 35.7 reduce-scatter.86
  719.0 37.5 reduce-scatter.104
  759.1 40.0 reduce-scatter.92
  801.7 33.6 reduce-scatter.108
  837.9 31.4 reduce-scatter.98
  871.9 31.4 reduce-scatter.112
  906.1 31.4 reduce-scatter.80
  940.1 31.4 reduce-scatter.100
  1023.5 33.6 reduce-scatter.106
  1060.8 35.8 reduce-scatter.110
  1100.1 34.9 reduce-scatter.114
  1137.4 31.4 reduce-scatter.102
  1234.5 37.6 all-reduce.52
  1275.7 68.1 reduce-scatter.174
  1347.3 66.5 reduce-scatter.176
  1417.4 66.8 reduce-scatter.178
  1487.8 67.0 reduce-scatter.172
  1558.3 66.7 reduce-scatter.150
  1628.6 66.5 reduce-scatter.152
  1698.7 66.7 reduce-scatter.154
  1768.9 66.5 reduce-scatter.148
  1838.7 60.9 reduce-scatter.166
  1903.3 60.9 reduce-scatter.168
  1967.5 60.8 reduce-scatter.164
  2032.1 61.0 reduce-scatter.170
  2096.6 64.5 reduce-scatter.142
  2165.1 64.3 reduce-scatter.144
  2232.8 64.4 reduce-scatter.140
  2301.1 64.3 reduce-scatter.146
  2368.7 60.8 reduce-scatter.124
  2433.1 60.8 reduce-scatter.126
  2497.2 60.9 reduce-scatter.128
  2561.8 60.9 reduce-scatter.130
  2626.0 62.2 reduce-scatter.116
  2692.1 62.4 reduce-scatter.118
  2757.9 62.4 reduce-scatter.120
  2824.2 62.4 reduce-scatter.122
  2889.9 63.8 reduce-scatter.156
  2957.6 63.6 reduce-scatter.158
  3024.7 63.7 reduce-scatter.160
  3092.3 63.7 reduce-scatter.162
  3159.6 67.1 reduce-scatter.132
  3230.2 67.0 reduce-scatter.134
  3300.7 67.2 reduce-scatter.136
  3371.6 67.2 reduce-scatter.138
